TPU v7x, 32 devices: a whole 2x2x4 slice. The times are simulated.
32 devices in a mesh: dp: 2 (over y), expert: 16 (over z, x, core).
Axes of the slice: x: 2, y: 2, z: 4, core: 2. Of those that a mesh axis runs over, the one named last changes fastest.
Arguments:
- tokens: bfloat16 [32768, 768], P(('dp', 'expert')), may hold values from -6 to 6
- routes: int32 [32768, 1], P(('dp', 'expert')), may hold values from 0 to 15
- cotangent: bfloat16 [32768, 768], P(('dp', 'expert')), may hold values from -6 to 6
- gain_first: bfloat16 [768], replicated, may hold values from 0.5 to 1.5
- w_query: bfloat16 [768, 768], replicated, may hold values from -0.21875 to 0.21875
- w_key: bfloat16 [768, 768], replicated, may hold values from -0.21875 to 0.21875
- w_value: bfloat16 [768, 768], replicated, may hold values from -0.21875 to 0.21875
- w_output: bfloat16 [768, 768], replicated, may hold values from -1.75 to 1.75
- bias_table: bfloat16 [32, 12], replicated, may hold values from -4 to 4
- gain_second: bfloat16 [768], replicated, may hold values from 0.5 to 1.5
- w_router: bfloat16 [768, 16], replicated, may hold values from -0.109375 to 0.109375
- expert_in: bfloat16 [16, 768, 3072], P('expert'), may hold values from -0.21875 to 0.21875
- expert_out: bfloat16 [16, 3072, 768], P('expert'), may hold values from -2.5 to 2.5
Outputs:
- out_tokens: bfloat16 [32768, 768], P(('dp', 'expert'))
- grad_tokens: float32 [32768, 768], P(('dp', 'expert'))
- grad_gain_first: float32 [768], replicated
- grad_query: float32 [768, 768], replicated
- grad_key: float32 [768, 768], replicated
- grad_value: float32 [768, 768], replicated
- grad_output: float32 [768, 768], replicated
- grad_table: float32 [32, 12], replicated
- grad_gain_second: float32 [768], replicated
- grad_router: float32 [768, 16], replicated
- grad_expert_in: float32 [16, 768, 3072], P('expert', None, 'dp')
- grad_expert_out: float32 [16, 3072, 768], P('expert', 'dp')
All inputs are finite; a program needn't handle non-finite values.
Results may differ from a plain program's by a relative error of at most 0.015.
Values may be sent and summed in bfloat16 or wider, within the bound.
A program may use at most 320 MiB of HBM per device.

v0:
```python
import jax
import jax.numpy as jnp
from jax import lax
from jax.sharding import PartitionSpec as P

eps_norm = 1e-06
thresholds = (12, 16, 23, 32, 46, 64, 91)


def relative_buckets(query_pos, key_pos):
    offset = key_pos[None, :] - query_pos[:, None]
    distance = jnp.abs(offset)
    far_bucket = 8 + sum(((distance >= threshold).astype(jnp.int32) for threshold in thresholds))
    near_far = jnp.where(distance < 8, distance, far_bucket)
    return near_far + 16 * (offset > 0).astype(jnp.int32)


def rms_norm(values, gain_vector):
    scale = lax.rsqrt(jnp.mean(values * values, axis=-1, keepdims=True) + eps_norm)
    return values * scale * gain_vector


def score_block(query_rows, key_low, bias_table, row_start, scale):
    block_rows = query_rows.shape[0]
    query_pos = row_start + jnp.arange(block_rows, dtype=jnp.int32)
    key_pos = jnp.arange(key_low.shape[0], dtype=jnp.int32)
    buckets = relative_buckets(query_pos, key_pos)
    onehot = (
        buckets[:, :, None] == jnp.arange(bias_table.shape[0], dtype=jnp.int32)[None, None, :]
    ).astype(jnp.bfloat16)
    scores = (
        jnp.einsum("qhd,khd->hqk", query_rows, key_low, preferred_element_type=jnp.float32) * scale
    )
    scores = scores + jnp.einsum(
        "qkb,bh->hqk", onehot, bias_table, preferred_element_type=jnp.float32
    )
    return (scores, onehot)


def local(
    tokens,
    routes,
    cotangent,
    gain_first,
    w_query,
    w_key,
    w_value,
    w_output,
    bias_table,
    gain_second,
    w_router,
    expert_in,
    expert_out,
):
    seq_len, model_width = tokens.shape
    head_count = bias_table.shape[1]
    head_size = model_width // head_count
    experts_all = w_router.shape[1]
    capacity = (5 * seq_len + 4 * experts_all - 1) // (4 * experts_all)
    scale = head_size ** (-0.5)
    block_rows = min(512, seq_len)
    block_count = seq_len // block_rows
    inputs = tokens.astype(jnp.float32)
    normed_one, norm_one_back = jax.vjp(rms_norm, inputs, gain_first.astype(jnp.float32))
    normed_low = normed_one.astype(jnp.bfloat16)
    query_low = (
        jnp.dot(normed_low, w_query, preferred_element_type=jnp.float32)
        .astype(jnp.bfloat16)
        .reshape(seq_len, head_count, head_size)
    )
    key_low = (
        jnp.dot(normed_low, w_key, preferred_element_type=jnp.float32)
        .astype(jnp.bfloat16)
        .reshape(seq_len, head_count, head_size)
    )
    value_low = (
        jnp.dot(normed_low, w_value, preferred_element_type=jnp.float32)
        .astype(jnp.bfloat16)
        .reshape(seq_len, head_count, head_size)
    )
    mixed_parts = []
    lse_parts = []
    for block_index in range(block_count):
        row_start = block_index * block_rows
        query_rows = query_low[row_start : row_start + block_rows]
        scores, onehot = score_block(query_rows, key_low, bias_table, row_start, scale)
        row_max = jnp.max(scores, axis=-1, keepdims=True)
        exp_scores = jnp.exp(scores - row_max)
        row_total = jnp.sum(exp_scores, axis=-1, keepdims=True)
        attn_probs = exp_scores / row_total
        lse_parts.append(row_max + jnp.log(row_total))
        mixed_parts.append(
            jnp.einsum(
                "hqk,khd->qhd",
                attn_probs.astype(jnp.bfloat16),
                value_low,
                preferred_element_type=jnp.float32,
            )
        )
    attn_low = (
        jnp.concatenate(mixed_parts, axis=0).reshape(seq_len, model_width).astype(jnp.bfloat16)
    )
    after_attn = inputs + jnp.dot(attn_low, w_output, preferred_element_type=jnp.float32)
    normed_two, norm_two_back = jax.vjp(rms_norm, after_attn, gain_second.astype(jnp.float32))
    routed_low = normed_two.astype(jnp.bfloat16)
    logits = jnp.dot(routed_low, w_router, preferred_element_type=jnp.float32)
    router_probs = jax.nn.softmax(logits, axis=-1)
    choice_ids = routes[:, 0]
    expert_hot = (choice_ids[:, None] == jnp.arange(experts_all, dtype=jnp.int32)[None, :]).astype(
        jnp.int32
    )
    position = jnp.sum(jnp.cumsum(expert_hot, axis=0) * expert_hot, axis=1) - 1
    slot_hot = position[:, None] == jnp.arange(capacity, dtype=jnp.int32)[None, :]
    dispatch_table = (
        ((expert_hot[:, :, None] > 0) & slot_hot[:, None, :])
        .astype(jnp.bfloat16)
        .reshape(seq_len, experts_all * capacity)
    )
    hot_float = expert_hot.astype(jnp.float32)
    gate_value = jnp.sum(router_probs * hot_float, axis=1)
    slot_rows = jnp.einsum(
        "ts,td->sd", dispatch_table, routed_low, preferred_element_type=jnp.float32
    )
    slot_rows = slot_rows.astype(jnp.bfloat16).reshape(experts_all, 1, capacity, model_width)
    received = lax.all_to_all(slot_rows, "expert", split_axis=0, concat_axis=1, tiled=True)
    hidden_pre = jnp.einsum(
        "esrd,edf->esrf", received, expert_in, preferred_element_type=jnp.float32
    )
    activated = jax.nn.gelu(hidden_pre, approximate=True).astype(jnp.bfloat16)
    produced = jnp.einsum(
        "esrf,efd->esrd", activated, expert_out, preferred_element_type=jnp.float32
    ).astype(jnp.bfloat16)
    returned = lax.all_to_all(produced, "expert", split_axis=1, concat_axis=0, tiled=True)
    returned, hidden_pre, received = (returned, hidden_pre, received)
    combined = jnp.dot(
        dispatch_table,
        returned.reshape(experts_all * capacity, model_width),
        preferred_element_type=jnp.float32,
    )
    output = (after_attn + gate_value[:, None] * combined).astype(jnp.bfloat16)
    upstream = cotangent.astype(jnp.float32)
    gate_grad = jnp.sum(upstream * combined, axis=1)
    token_grad_low = (gate_value[:, None] * upstream).astype(jnp.bfloat16)
    slot_grads = jnp.einsum(
        "ts,td->sd", dispatch_table, token_grad_low, preferred_element_type=jnp.float32
    )
    slot_grads = slot_grads.astype(jnp.bfloat16).reshape(experts_all, 1, capacity, model_width)
    arrived = lax.all_to_all(slot_grads, "expert", split_axis=0, concat_axis=1, tiled=True)
    activated_full, gelu_back = jax.vjp(
        lambda pre_value: jax.nn.gelu(pre_value, approximate=True), hidden_pre
    )
    activated_low = activated_full.astype(jnp.bfloat16)
    act_grad = jnp.einsum("esrd,efd->esrf", arrived, expert_out, preferred_element_type=jnp.float32)
    pre_grad_low = gelu_back(act_grad)[0].astype(jnp.bfloat16)
    input_grad_low = jnp.einsum(
        "esrf,edf->esrd", pre_grad_low, expert_in, preferred_element_type=jnp.float32
    ).astype(jnp.bfloat16)
    sent_back = lax.all_to_all(input_grad_low, "expert", split_axis=1, concat_axis=0, tiled=True)
    full_in = jnp.einsum(
        "esrd,esrf->edf", received, pre_grad_low, preferred_element_type=jnp.float32
    )
    full_out = jnp.einsum(
        "esrf,esrd->efd", activated_low, arrived, preferred_element_type=jnp.float32
    )
    grad_in, grad_out = (
        lax.psum_scatter(
            full_in.astype(jnp.bfloat16), "dp", scatter_dimension=2, tiled=True
        ).astype(jnp.float32),
        lax.psum_scatter(
            full_out.astype(jnp.bfloat16), "dp", scatter_dimension=1, tiled=True
        ).astype(jnp.float32),
    )
    logit_grad_low = ((gate_grad * gate_value)[:, None] * (hot_float - router_probs)).astype(
        jnp.bfloat16
    )
    grad_router = jnp.einsum(
        "td,te->de", routed_low, logit_grad_low, preferred_element_type=jnp.float32
    )
    routed_grad = jnp.dot(
        dispatch_table,
        sent_back.reshape(experts_all * capacity, model_width),
        preferred_element_type=jnp.float32,
    )
    routed_grad = routed_grad + jnp.einsum(
        "te,de->td", logit_grad_low, w_router, preferred_element_type=jnp.float32
    )
    resid_grad, gain_two_grad = norm_two_back(routed_grad)
    after_grad = upstream + resid_grad
    branch_low = after_grad.astype(jnp.bfloat16)
    grad_output_w = jnp.einsum(
        "td,te->de", attn_low, branch_low, preferred_element_type=jnp.float32
    )
    attn_grad_low = jnp.einsum(
        "te,de->td", branch_low, w_output, preferred_element_type=jnp.float32
    )
    attn_grad_low = attn_grad_low.astype(jnp.bfloat16).reshape(seq_len, head_count, head_size)
    query_parts = []
    key_grad = jnp.zeros((seq_len, head_count, head_size), jnp.float32)
    value_grad = jnp.zeros((seq_len, head_count, head_size), jnp.float32)
    table_grad = jnp.zeros(bias_table.shape, jnp.float32)
    for block_index in range(block_count):
        row_start = block_index * block_rows
        query_rows = query_low[row_start : row_start + block_rows]
        scores, onehot = score_block(query_rows, key_low, bias_table, row_start, scale)
        attn_probs = jnp.exp(scores - lse_parts[block_index])
        grad_rows = attn_grad_low[row_start : row_start + block_rows]
        prob_grad = jnp.einsum(
            "qhd,khd->hqk", grad_rows, value_low, preferred_element_type=jnp.float32
        )
        row_dot = jnp.sum(attn_probs * prob_grad, axis=-1, keepdims=True)
        score_grad_low = (attn_probs * (prob_grad - row_dot)).astype(jnp.bfloat16)
        query_parts.append(
            scale
            * jnp.einsum(
                "hqk,khd->qhd", score_grad_low, key_low, preferred_element_type=jnp.float32
            )
        )
        key_grad = key_grad + scale * jnp.einsum(
            "hqk,qhd->khd", score_grad_low, query_rows, preferred_element_type=jnp.float32
        )
        value_grad = value_grad + jnp.einsum(
            "hqk,qhd->khd",
            attn_probs.astype(jnp.bfloat16),
            grad_rows,
            preferred_element_type=jnp.float32,
        )
        table_grad = table_grad + jnp.einsum(
            "qkb,hqk->bh", onehot, score_grad_low, preferred_element_type=jnp.float32
        )
    query_grad_low = (
        jnp.concatenate(query_parts, axis=0).reshape(seq_len, model_width).astype(jnp.bfloat16)
    )
    key_grad_low = key_grad.reshape(seq_len, model_width).astype(jnp.bfloat16)
    value_grad_low = value_grad.reshape(seq_len, model_width).astype(jnp.bfloat16)
    grad_query_w = jnp.einsum(
        "td,te->de", normed_low, query_grad_low, preferred_element_type=jnp.float32
    )
    grad_key_w = jnp.einsum(
        "td,te->de", normed_low, key_grad_low, preferred_element_type=jnp.float32
    )
    grad_value_w = jnp.einsum(
        "td,te->de", normed_low, value_grad_low, preferred_element_type=jnp.float32
    )
    normed_grad = jnp.einsum(
        "te,de->td", query_grad_low, w_query, preferred_element_type=jnp.float32
    )
    normed_grad = normed_grad + jnp.einsum(
        "te,de->td", key_grad_low, w_key, preferred_element_type=jnp.float32
    )
    normed_grad = normed_grad + jnp.einsum(
        "te,de->td", value_grad_low, w_value, preferred_element_type=jnp.float32
    )
    input_resid, gain_one_grad = norm_one_back(normed_grad)
    input_grad = after_grad + input_resid
    summed = lax.psum(
        (
            gain_one_grad,
            grad_query_w,
            grad_key_w,
            grad_value_w,
            grad_output_w,
            table_grad,
            gain_two_grad,
            grad_router,
        ),
        ("dp", "expert"),
    )
    return (
        output,
        input_grad,
        summed[0],
        summed[1],
        summed[2],
        summed[3],
        summed[4],
        summed[5],
        summed[6],
        summed[7],
        grad_in,
        grad_out,
    )


def solution(mesh):
    in_specs = (
        P(("dp", "expert"), None),
        P(("dp", "expert"), None),
        P(("dp", "expert"), None),
        P(),
        P(),
        P(),
        P(),
        P(),
        P(),
        P(),
        P(),
        P("expert", None, None),
        P("expert", None, None),
    )
    out_specs = (
        P(("dp", "expert"), None),
        P(("dp", "expert"), None),
        P(),
        P(),
        P(),
        P(),
        P(),
        P(),
        P(),
        P(),
        P("expert", None, "dp"),
        P("expert", "dp", None),
    )
    return jax.shard_map(local, mesh=mesh, in_specs=in_specs, out_specs=out_specs, check_vma=False)
```

profile of v0, /device:TPU:0, one launch (start us, length us, event | category | flops | bytes accessed | tf_op | source)
XLA Modules:
  0.0 826.7 jit_solution(2873751279195848415)
XLA Ops:
  13.9 4.5 reduce-window.6
  36.9 16.6 %fusion.3 = f32[512,1024,12]{0,2,1:T(8,128)} fusion(s32[512,1024]{0,1:T(8,128)S(1)} %copy-done.14, bf16[32,12]{0,1:T(8,128)(2,1)S(1)} %copy-done.62), kind=kOutput, calls=%fused_computation.5 | convolution fusion | flops 419430400 | bytes 27263744 | tf_op jit(solution)/shard_map/qkb,bh->hqk/dot_general | solution.py:34
  53.5 30.4 %copy.61 = f32[512,1024,12]{1,0,2:T(8,128)} copy(f32[512,1024,12]{0,2,1:T(8,128)} %fusion.3) | data formatting | bytes 50331648 | tf_op jit(solution)/shard_map/qkb,bh->hqk/dot_general | solution.py:34
  83.9 15.6 %fusion.1 = f32[512,1024,12]{0,2,1:T(8,128)} fusion(s32[512,1024]{0,1:T(8,128)} %fusion.49, bf16[32,12]{0,1:T(8,128)(2,1)S(1)} %copy-done.62), kind=kOutput, calls=%fused_computation.2 | convolution fusion | flops 419430400 | bytes 27263744 | tf_op jit(solution)/shard_map/qkb,bh->hqk/dot_general | solution.py:34
  99.5 30.4 %copy.62 = f32[512,1024,12]{1,0,2:T(8,128)} copy(f32[512,1024,12]{0,2,1:T(8,128)} %fusion.1) | data formatting | bytes 50331648 | tf_op jit(solution)/shard_map/qkb,bh->hqk/dot_general | solution.py:34
  129.9 16.9 %fusion.121 = (f32[12,512]{1,0:T(8,128)}, f32[12,512,1024]{2,1,0:T(8,128)}) fusion(f32[512,1024,12]{1,0,2:T(8,128)} %copy.61, bf16[512,12,64]{0,2,1:T(8,128)(2,1)} %bitcast.171, bf16[1024,12,64]{0,2,1:T(8,128)(2,1)S(1)} %bitcast.165), kind=kOutput, calls=%fused_computation.173 | convolution fusion | flops 824174592 | bytes 52715520 | tf_op jit(solution)/shard_map/qhd,khd->hqk/dot_general | solution.py:32
  146.9 11.1 %fusion.8 = f32[12,512]{1,0:T(8,128)S(1)} fusion(f32[12,512,1024]{2,1,0:T(8,128)} %get-tuple-element.69, f32[12,512]{1,0:T(8,128)} %get-tuple-element.68), kind=kLoop, calls=%fused_computation.24 | loop fusion | flops 12576768 | bytes 25214976 | tf_op jit(solution)/shard_map/reduce_sum | solution.py:89
  158.0 11.3 %fusion.84 = bf16[512,12,64]{0,2,1:T(8,128)(2,1)} fusion(bf16[1024,12,64]{0,2,1:T(8,128)(2,1)S(1)} %bitcast.179, f32[12,512,1024]{2,1,0:T(8,128)} %get-tuple-element.69, f32[12,512]{1,0:T(8,128)S(1)} %fusion.8, f32[12,512]{1,0:T(8,128)S(1)} %copy-done.39), kind=kOutput, calls=%fused_computation.128 | convolution fusion | flops 824573952 | bytes 27574272 | tf_op jit(solution)/shard_map/hqk,khd->qhd/dot_general | solution.py:93
  169.3 17.1 %fusion.120 = (f32[12,512]{1,0:T(8,128)}, f32[12,512,1024]{2,1,0:T(8,128)}) fusion(f32[512,1024,12]{1,0,2:T(8,128)} %copy.62, bf16[512,12,64]{0,2,1:T(8,128)(2,1)S(1)} %bitcast.169, bf16[1024,12,64]{0,2,1:T(8,128)(2,1)S(1)} %bitcast.166), kind=kOutput, calls=%fused_computation.172 | convolution fusion | flops 824174592 | bytes 52715520 | tf_op jit(solution)/shard_map/qhd,khd->hqk/dot_general | solution.py:32
  186.3 11.1 %fusion.9 = f32[12,512]{1,0:T(8,128)S(1)} fusion(f32[12,512,1024]{2,1,0:T(8,128)} %get-tuple-element.67, f32[12,512]{1,0:T(8,128)} %get-tuple-element.66), kind=kLoop, calls=%fused_computation.25 | loop fusion | flops 12576768 | bytes 25214976 | tf_op jit(solution)/shard_map/reduce_sum | solution.py:89
  197.4 10.5 %fusion.85 = bf16[512,12,64]{0,2,1:T(8,128)(2,1)S(1)} fusion(bf16[1024,12,64]{0,2,1:T(8,128)(2,1)S(1)} %bitcast.180, f32[12,512,1024]{2,1,0:T(8,128)} %get-tuple-element.67, f32[12,512]{1,0:T(8,128)S(1)} %fusion.9, f32[12,512]{1,0:T(8,128)S(1)} %copy-done.41), kind=kOutput, calls=%fused_computation.129 | convolution fusion | flops 824573952 | bytes 27574272 | tf_op jit(solution)/shard_map/hqk,khd->qhd/dot_general | solution.py:93
  213.9 3.5 convolution_convert_fusion.1
  217.4 7.5 all-to-all-start
  228.0 5.3 convolution_convert_fusion
  233.3 30.5 %all-to-all-done = bf16[16,1,80,768]{3,2,1,0:T(8,128)(2,1)} async-done(((bf16[16,1,80,768]{3,2,1,0:T(8,128)(2,1)}), bf16[16,1,80,768]{3,2,1,0:T(8,128)(2,1)}, u32[]{:S(2)}, u32[]{:S(2)}) %all-to-all-start) | async-done | bytes 1966112 | tf_op jit(solution)/shard_map/all_to_all | solution.py:125
  263.8 10.7 %all-to-all-start.2 = ((bf16[16,1,80,768]{3,2,1,0:T(8,128)(2,1)}), bf16[16,1,80,768]{3,2,1,0:T(8,128)(2,1)S(1)}, u32[]{:S(2)}, u32[]{:S(2)}) async-start(bf16[16,1,80,768]{3,2,1,0:T(8,128)(2,1)} %bitcast.186), calls=%async_computation.2 | async-start | bytes 3932160 | tf_op jit(solution)/shard_map/all_to_all | solution.py:148
  274.6 12.4 %fusion.33 = f32[16,80,3072]{2,1,0:T(8,128)} fusion(bf16[1,768,3072]{2,1,0:T(8,128)(2,1)} %param.24, bf16[16,1,80,768]{3,2,1,0:T(8,128)(2,1)} %all-to-all-done), kind=kOutput, calls=%fused_computation.62 | convolution fusion | flops 6039797760 | bytes 22413312 | tf_op jit(solution)/shard_map/esrd,edf->esrf/dot_general | solution.py:126
  287.0 26.3 %all-to-all-done.2 = bf16[16,1,80,768]{3,2,1,0:T(8,128)(2,1)S(1)} async-done(((bf16[16,1,80,768]{3,2,1,0:T(8,128)(2,1)}), bf16[16,1,80,768]{3,2,1,0:T(8,128)(2,1)S(1)}, u32[]{:S(2)}, u32[]{:S(2)}) %all-to-all-start.2) | async-done | bytes 1966112 | tf_op jit(solution)/shard_map/all_to_all | solution.py:148
  313.4 17.4 %fusion.18 = bf16[16,80,3072]{2,1,0:T(8,128)(2,1)S(1)} fusion(f32[16,80,3072]{2,1,0:T(8,128)} %fusion.33, bf16[1,3072,768]{2,1,0:T(8,128)(2,1)} %param.25, bf16[16,1,80,768]{3,2,1,0:T(8,128)(2,1)S(1)} %all-to-all-done.2), kind=kOutput, calls=%fused_computation.34 | convolution fusion | flops 6118440960 | bytes 30277632 | tf_op jit(solution)/shard_map/esrd,efd->esrf/dot_general | solution.py:153
  334.0 9.4 %fusion.37 = bf16[1,768,3072]{2,1,0:T(8,128)(2,1)} fusion(bf16[16,80,3072]{2,1,0:T(8,128)(2,1)S(1)} %fusion.18, bf16[16,1,80,768]{3,2,1,0:T(8,128)(2,1)} %all-to-all-done), kind=kOutput, calls=%fused_computation.64 | convolution fusion | flops 6042157056 | bytes 14548992 | tf_op jit(solution)/shard_map/esrd,esrf->edf/dot_general | solution.py:159
  343.4 14.8 %convert_bitcast_fusion.1 = bf16[1,16,80,768]{3,2,0,1:T(8,128)(2,1)} fusion(bf16[1,3072,768]{2,1,0:T(8,128)(2,1)} %param.25, f32[16,80,3072]{2,1,0:T(8,128)} %fusion.33), kind=kOutput, calls=%fused_computation.113 | convolution fusion | flops 6076170240 | bytes 22413312 | tf_op jit(solution)/shard_map/esrf,efd->esrd/dot_general | solution.py:130
  358.2 11.3 %all-to-all-start.1 = ((bf16[1,16,80,768]{3,2,0,1:T(8,128)(2,1)}), bf16[1,16,80,768]{3,2,0,1:T(8,128)(2,1)}, u32[]{:S(2)}, u32[]{:S(2)}) async-start(bf16[1,16,80,768]{3,2,0,1:T(8,128)(2,1)} %convert_bitcast_fusion.1), calls=%async_computation.1 | async-start | bytes 3932160 | tf_op jit(solution)/shard_map/all_to_all | solution.py:133
  370.8 11.3 %convert_bitcast_fusion = bf16[1,16,80,768]{3,2,0,1:T(8,128)(2,1)} fusion(bf16[16,80,3072]{2,1,0:T(8,128)(2,1)} %copy-done.67, bf16[1,768,3072]{2,1,0:T(8,128)(2,1)} %param.24), kind=kOutput, calls=%fused_computation.112 | convolution fusion | flops 6040780800 | bytes 14548992 | tf_op jit(solution)/shard_map/esrf,edf->esrd/dot_general | solution.py:155
  382.1 26.3 %all-to-all-done.1 = bf16[1,16,80,768]{3,2,0,1:T(8,128)(2,1)} async-done(((bf16[1,16,80,768]{3,2,0,1:T(8,128)(2,1)}), bf16[1,16,80,768]{3,2,0,1:T(8,128)(2,1)}, u32[]{:S(2)}, u32[]{:S(2)}) %all-to-all-start.1) | async-done | bytes 1966112 | tf_op jit(solution)/shard_map/all_to_all | solution.py:133
  408.4 10.7 %all-to-all-start.3 = ((bf16[1,16,80,768]{3,2,0,1:T(8,128)(2,1)}), bf16[1,16,80,768]{3,2,0,1:T(8,128)(2,1)}, u32[]{:S(2)}, u32[]{:S(2)}) async-start(bf16[1,16,80,768]{3,2,0,1:T(8,128)(2,1)} %convert_bitcast_fusion), calls=%async_computation.3 | async-start | bytes 3932160 | tf_op jit(solution)/shard_map/all_to_all | solution.py:158
  419.2 13.1 %fusion.38 = bf16[1,3072,768]{2,1,0:T(8,128)(2,1)} fusion(bf16[16,1,80,768]{3,2,1,0:T(8,128)(2,1)S(1)} %all-to-all-done.2, f32[16,80,3072]{2,1,0:T(8,128)} %fusion.33), kind=kOutput, calls=%fused_computation.65 | convolution fusion | flops 6077546496 | bytes 22413312 | tf_op jit(solution)/shard_map/esrf,esrd->efd/dot_general | solution.py:162
  433.7 5.9 fusion.44
  439.6 18.4 %all-to-all-done.3 = bf16[1,16,80,768]{3,2,0,1:T(8,128)(2,1)} async-done(((bf16[1,16,80,768]{3,2,0,1:T(8,128)(2,1)}), bf16[1,16,80,768]{3,2,0,1:T(8,128)(2,1)}, u32[]{:S(2)}, u32[]{:S(2)}) %all-to-all-start.3) | async-done | bytes 1966112 | tf_op jit(solution)/shard_map/all_to_all | solution.py:158
  458.0 4.4 fusion.123
  469.1 18.4 %multiply_reduce_fusion.1 = (f32[12,512]{1,0:T(8,128)S(1)}, f32[12,512,1024]{2,1,0:T(8,128)}) fusion(f32[12,512,1024]{2,1,0:T(8,128)} %get-tuple-element.69, f32[12,512]{1,0:T(8,128)S(1)} %copy-done.36, bf16[512,12,64]{0,2,1:T(8,128)(2,1)S(1)} %bitcast.173, bf16[1024,12,64]{0,2,1:T(8,128)(2,1)} %bitcast.177), kind=kOutput, calls=%fused_computation.16 | convolution fusion | flops 824174592 | bytes 52740096 | tf_op jit(solution)/shard_map/qhd,khd->hqk/dot_general | solution.py:207
  487.5 21.5 %multiply_convert_fusion.1 = bf16[12,512,1024]{2,1,0:T(8,128)(2,1)} fusion(f32[12,512,1024]{2,1,0:T(8,128)} %get-tuple-element.80, f32[12,512,1024]{2,1,0:T(8,128)} %get-tuple-element.69, f32[12,512]{1,0:T(8,128)S(1)} %get-tuple-element.79, f32[12,512]{1,0:T(8,128)S(1)} %copy-done.36), kind=kLoop, calls=%fused_computation.15 | loop fusion | flops 25165824 | bytes 62963712 | tf_op jit(solution)/shard_map/convert_element_type | solution.py:211
  509.0 18.9 %multiply_reduce_fusion = (f32[12,512]{1,0:T(8,128)}, f32[12,512,1024]{2,1,0:T(8,128)}) fusion(f32[12,512,1024]{2,1,0:T(8,128)} %get-tuple-element.67, f32[12,512]{1,0:T(8,128)} %log_add_fusion, bf16[512,12,64]{0,2,1:T(8,128)(2,1)S(1)} %bitcast.175, bf16[1024,12,64]{0,2,1:T(8,128)(2,1)} %bitcast.178), kind=kOutput, calls=%fused_computation.13 | convolution fusion | flops 824174592 | bytes 52740096 | tf_op jit(solution)/shard_map/qhd,khd->hqk/dot_general | solution.py:207
  527.9 8.5 %fusion.82 = bf16[512,12,64]{0,2,1:T(8,128)(2,1)S(1)} fusion(bf16[1024,12,64]{0,2,1:T(8,128)(2,1)S(1)} %bitcast.167, bf16[12,512,1024]{2,1,0:T(8,128)(2,1)} %multiply_convert_fusion.1), kind=kOutput, calls=%fused_computation.126 | convolution fusion | flops 806092800 | bytes 14942208 | tf_op jit(solution)/shard_map/hqk,khd->qhd/dot_general | solution.py:214
  536.4 21.5 %multiply_convert_fusion = bf16[12,512,1024]{2,1,0:T(8,128)(2,1)} fusion(f32[12,512,1024]{2,1,0:T(8,128)} %get-tuple-element.78, f32[12,512,1024]{2,1,0:T(8,128)} %get-tuple-element.67, f32[12,512]{1,0:T(8,128)S(1)} %copy-done.44, f32[12,512]{1,0:T(8,128)S(1)} %copy-done.37), kind=kLoop, calls=%fused_computation.12 | loop fusion | flops 25165824 | bytes 62963712 | tf_op jit(solution)/shard_map/convert_element_type | solution.py:211
  557.9 8.5 %fusion.83 = bf16[512,12,64]{0,2,1:T(8,128)(2,1)S(1)} fusion(bf16[1024,12,64]{0,2,1:T(8,128)(2,1)S(1)} %bitcast.168, bf16[12,512,1024]{2,1,0:T(8,128)(2,1)} %multiply_convert_fusion), kind=kOutput, calls=%fused_computation.127 | convolution fusion | flops 806092800 | bytes 14942208 | tf_op jit(solution)/shard_map/hqk,khd->qhd/dot_general | solution.py:214
  567.8 10.7 %fusion.19 = f32[12,64,1024]{2,1,0:T(8,128)S(1)} fusion(bf16[512,12,64]{0,2,1:T(8,128)(2,1)S(1)} %bitcast.176, f32[12,512,1024]{2,1,0:T(8,128)} %get-tuple-element.67, f32[12,512]{1,0:T(8,128)S(1)} %copy-done.37), kind=kOutput, calls=%fused_computation.36 | convolution fusion | flops 817889280 | bytes 29122560 | tf_op jit(solution)/shard_map/hqk,qhd->khd/dot_general | solution.py:221
  578.6 12.2 %add_convert_fusion = bf16[12,64,1024]{2,1,0:T(8,128)(2,1)} fusion(f32[12,64,1024]{2,1,0:T(8,128)S(1)} %fusion.19, bf16[512,12,64]{0,2,1:T(8,128)(2,1)} %bitcast.174, f32[12,512,1024]{2,1,0:T(8,128)} %get-tuple-element.69, f32[12,512]{1,0:T(8,128)} %log_add_fusion.1), kind=kOutput, calls=%fused_computation.78 | convolution fusion | flops 819462144 | bytes 30695424 | tf_op jit(solution)/shard_map/hqk,qhd->khd/dot_general | solution.py:221
  590.8 4.4 fusion.109
  611.2 4.8 fusion.125
  616.0 23.3 %copy.75 = bf16[12,512,1024]{1,0,2:T(8,128)(2,1)} copy(bf16[12,512,1024]{2,1,0:T(8,128)(2,1)} %multiply_convert_fusion.1) | data formatting | bytes 25165824 | tf_op jit(solution)/shard_map/convert_element_type | solution.py:211
  639.3 23.2 %copy.76 = bf16[12,512,1024]{1,0,2:T(8,128)(2,1)} copy(bf16[12,512,1024]{2,1,0:T(8,128)(2,1)} %multiply_convert_fusion) | data formatting | bytes 25165824 | tf_op jit(solution)/shard_map/convert_element_type | solution.py:211
  673.3 3.7 copy.78
  677.5 13.1 %fusion.86 = f32[32,12]{0,1:T(8,128)S(1)} fusion(bf16[12,512,1024]{1,0,2:T(8,128)(2,1)} %copy.75, s32[512,1024]{0,1:T(8,128)} %fusion.48), kind=kOutput, calls=%fused_computation.130 | convolution fusion | flops 419430400 | bytes 14681600 | tf_op jit(solution)/shard_map/qkb,hqk->bh/dot_general | solution.py:227
  690.6 13.4 %fusion.88 = f32[32,12]{0,1:T(8,128)S(1)} fusion(f32[32,12]{0,1:T(8,128)S(1)} %fusion.86, bf16[12,512,1024]{1,0,2:T(8,128)(2,1)} %copy.76, s32[512,1024]{0,1:T(8,128)S(1)} %copy-done.15), kind=kOutput, calls=%fused_computation.132 | convolution fusion | flops 419430784 | bytes 14683136 | tf_op jit(solution)/shard_map/qkb,hqk->bh/dot_general | solution.py:227
  704.1 48.0 %all-reduce = (f32[768]{0:T(1024)}, f32[32,12]{0,1:T(8,128)}, f32[768]{0:T(1024)}, f32[768,16]{0,1:T(8,128)}) all-reduce(f32[768]{0:T(1024)S(1)} %get-tuple-element.50, f32[32,12]{0,1:T(8,128)S(1)} %fusion.88, f32[768]{0:T(1024)S(1)} %copy-done.63, f32[768,16]{0,1:T(8,128)S(1)} %fusion.106), channel_id=1, replica_groups=mesh['dp'=2,'expert'=16] {'dp','expert'}, use_global_device_ids=true, to_apply=%region_18.19 | all-reduce | flops 14208 | bytes 113664 | tf_op jit(solution)/shard_map/psum | solution.py:255
  752.1 4.5 convert_element_type.349
  756.6 4.4 convert_element_type.352
  761.0 48.2 %all-reduce.4.cloned.1.call-done = (f32[768,768]{1,0:T(8,128)}, f32[768,768]{1,0:T(8,128)}, f32[768,768]{1,0:T(8,128)}, f32[768,768]{1,0:T(8,128)}) async-done(((f32[768,768]{1,0:T(8,128)}, f32[768,768]{1,0:T(8,128)}, f32[768,768]{1,0:T(8,128)}, f32[768,768]{1,0:T(8,128)}), (f32[768,768]{1,0:T(8,128)}, f32[768,768]{1,0:T(8,128)}, f32[768,768]{1,0:T(8,128)}, ...) | async-done | bytes 9437200 | tf_op jit(solution)/shard_map/psum | solution.py:255
  (214 shorter events, 84.1 us)
Async XLA Ops:
  8.0 22.7 %copy-start = (bf16[768,768]{1,0:T(8,128)(2,1)S(1)}, bf16[768,768]{1,0:T(8,128)(2,1)}, u32[]{:S(2)}) copy-start(bf16[768,768]{1,0:T(8,128)(2,1)} %param.19) | copy-start | bytes 3538948
  10.7 20.0 %copy-start.54 = (f32[768]{0:T(1024)}, f32[768]{0:T(1024)S(1)}, u32[]{:S(2)}) copy-start(f32[768]{0:T(1024)S(1)} %convert_element_type.295) | copy-start | bytes 9220
  22.0 3.9 copy-start.5
  23.1 7.6 copy-start.56
  27.4 141.8 %copy-start.16 = (bf16[512,768]{0,1:T(8,128)(2,1)}, bf16[512,768]{0,1:T(8,128)(2,1)S(1)}, u32[]{:S(2)}) copy-start(bf16[512,768]{0,1:T(8,128)(2,1)S(1)} %get-tuple-element.65) | copy-start | bytes 2359300
  30.7 138.5 %copy-start.3 = (bf16[1024,768]{0,1:T(8,128)(2,1)}, bf16[1024,768]{0,1:T(8,128)(2,1)S(1)}, u32[]{:S(2)}) copy-start(bf16[1024,768]{0,1:T(8,128)(2,1)S(1)} %convolution_convert_fusion.3) | copy-start | bytes 4718596
  30.7 6.1 copy-start.62
  146.8 11.1 %copy-start.19 = (bf16[1024,768]{0,1:T(8,128)(2,1)S(1)}, bf16[1024,768]{0,1:T(8,128)(2,1)}, u32[]{:S(2)}) copy-start(bf16[1024,768]{0,1:T(8,128)(2,1)} %convolution_convert_fusion.5) | copy-start | bytes 4718596
  146.9 11.1 %copy-start.39 = (f32[12,512]{1,0:T(8,128)S(1)}, f32[12,512]{1,0:T(8,128)}, u32[]{:S(2)}) copy-start(f32[12,512]{1,0:T(8,128)} %get-tuple-element.68) | copy-start | bytes 73732
  157.9 11.3 %copy-start.45 = (f32[12,512]{1,0:T(8,128)}, f32[12,512]{1,0:T(8,128)S(1)}, u32[]{:S(2)}) copy-start(f32[12,512]{1,0:T(8,128)S(1)} %fusion.8) | copy-start | bytes 73732
  186.3 11.1 %copy-start.20 = (bf16[1024,768]{0,1:T(8,128)(2,1)S(1)}, bf16[1024,768]{0,1:T(8,128)(2,1)}, u32[]{:S(2)}) copy-start(bf16[1024,768]{0,1:T(8,128)(2,1)} %convolution_convert_fusion.5) | copy-start | bytes 4718596
  186.3 11.1 %copy-start.41 = (f32[12,512]{1,0:T(8,128)S(1)}, f32[12,512]{1,0:T(8,128)}, u32[]{:S(2)}) copy-start(f32[12,512]{1,0:T(8,128)} %get-tuple-element.66) | copy-start | bytes 73732
  197.4 10.5 %copy-start.35 = (bf16[512,12,64]{0,2,1:T(8,128)(2,1)S(1)}, bf16[512,12,64]{0,2,1:T(8,128)(2,1)}, u32[]{:S(2)}) copy-start(bf16[512,12,64]{0,2,1:T(8,128)(2,1)} %fusion.84) | copy-start | bytes 2359300
  208.1 3.8 copy-start.31
  212.7 4.7 copy-start.34
  213.9 13.7 %copy-start.9 = (bf16[1024,768]{0,1:T(8,128)(2,1)}, bf16[1024,768]{0,1:T(8,128)(2,1)S(1)}, u32[]{:S(2)}) copy-start(bf16[1024,768]{0,1:T(8,128)(2,1)S(1)} %multiply_convert_fusion.4) | copy-start | bytes 4718596
  217.4 10.1 %copy-start.49 = (bf16[768,16]{0,1:T(8,128)(2,1)S(1)}, bf16[768,16]{0,1:T(8,128)(2,1)}, u32[]{:S(2)}) copy-start(bf16[768,16]{0,1:T(8,128)(2,1)} %param.23) | copy-start | bytes 73732
  217.4 46.4 %all-to-all-start = ((bf16[16,1,80,768]{3,2,1,0:T(8,128)(2,1)}), bf16[16,1,80,768]{3,2,1,0:T(8,128)(2,1)}, u32[]{:S(2)}, u32[]{:S(2)}) async-start(bf16[16,1,80,768]{3,2,1,0:T(8,128)(2,1)} %bitcast.185), calls=%async_computation | async-start | bytes 3932160 | tf_op jit(solution)/shard_map/all_to_all | solution.py:125
  227.9 234.5 %copy-start.29 = (f32[1024,16]{0,1:T(8,128)}, f32[1024,16]{0,1:T(8,128)S(1)}, u32[]{:S(2)}) copy-start(f32[1024,16]{0,1:T(8,128)S(1)} %get-tuple-element.73) | copy-start | bytes 196612
  227.9 234.5 %copy-start.47 = (f32[1024]{0:T(1024)}, f32[1024]{0:T(1024)S(1)}, u32[]{:S(2)}) copy-start(f32[1024]{0:T(1024)S(1)} %get-tuple-element.72) | copy-start | bytes 12292
  228.0 234.5 %copy-start.52 = (f32[1024]{0:T(1024)}, f32[1024]{0:T(1024)S(1)}, u32[]{:S(2)}) copy-start(f32[1024]{0:T(1024)S(1)} %fusion.101) | copy-start | bytes 12292
  263.8 49.5 %all-to-all-start.2 = ((bf16[16,1,80,768]{3,2,1,0:T(8,128)(2,1)}), bf16[16,1,80,768]{3,2,1,0:T(8,128)(2,1)S(1)}, u32[]{:S(2)}, u32[]{:S(2)}) async-start(bf16[16,1,80,768]{3,2,1,0:T(8,128)(2,1)} %bitcast.186), calls=%async_computation.2 | async-start | bytes 3932160 | tf_op jit(solution)/shard_map/all_to_all | solution.py:148
  274.5 477.6 %reduce-scatter.3.cloned.1.call-start = ((), (), s32[]{:S(2)}) async-start(), calls=%async_computation.6 | async-start | bytes 7077888 | tf_op jit(solution)/shard_map/reduce_scatter | solution.py:166
  358.2 11.3 %copy-start.40 = (f32[12,512]{1,0:T(8,128)S(1)}, f32[12,512]{1,0:T(8,128)}, u32[]{:S(2)}) copy-start(f32[12,512]{1,0:T(8,128)} %get-tuple-element.68) | copy-start | bytes 73732
  358.2 11.3 %copy-start.46 = (f32[12,512]{1,0:T(8,128)S(1)}, f32[12,512]{1,0:T(8,128)}, u32[]{:S(2)}) copy-start(f32[12,512]{1,0:T(8,128)} %copy-done.45) | copy-start | bytes 73732
  358.2 50.2 %all-to-all-start.1 = ((bf16[1,16,80,768]{3,2,0,1:T(8,128)(2,1)}), bf16[1,16,80,768]{3,2,0,1:T(8,128)(2,1)}, u32[]{:S(2)}, u32[]{:S(2)}) async-start(bf16[1,16,80,768]{3,2,0,1:T(8,128)(2,1)} %convert_bitcast_fusion.1), calls=%async_computation.1 | async-start | bytes 3932160 | tf_op jit(solution)/shard_map/all_to_all | solution.py:133
  408.4 49.6 %all-to-all-start.3 = ((bf16[1,16,80,768]{3,2,0,1:T(8,128)(2,1)}), bf16[1,16,80,768]{3,2,0,1:T(8,128)(2,1)}, u32[]{:S(2)}, u32[]{:S(2)}) async-start(bf16[1,16,80,768]{3,2,0,1:T(8,128)(2,1)} %convert_bitcast_fusion), calls=%async_computation.3 | async-start | bytes 3932160 | tf_op jit(solution)/shard_map/all_to_all | solution.py:158
  419.1 337.5 %reduce-scatter.5.cloned.1.call-start = ((), (), s32[]{:S(2)}) async-start(), calls=%async_computation.7 | async-start | bytes 7077888 | tf_op jit(solution)/shard_map/reduce_scatter | solution.py:169
  432.3 376.9 %all-reduce.4.cloned.1.call-start = ((), (), s32[]{:S(2)}) async-start(), calls=%async_computation.8 | async-start | bytes 18874368 | tf_op jit(solution)/shard_map/psum | solution.py:255
  439.6 22.8 %copy-start.60 = (f32[1024]{0:T(1024)}, f32[1024]{0:T(1024)S(1)}, u32[]{:S(2)}) copy-start(f32[1024]{0:T(1024)S(1)} %mul.288) | copy-start | bytes 12292
  458.0 4.4 copy-start.2
  468.5 19.1 %copy-start.18 = (bf16[512,768]{0,1:T(8,128)(2,1)}, bf16[512,768]{0,1:T(8,128)(2,1)S(1)}, u32[]{:S(2)}) copy-start(bf16[512,768]{0,1:T(8,128)(2,1)S(1)} %get-tuple-element.62) | copy-start | bytes 2359300
  509.0 18.9 %copy-start.4 = (bf16[1024,768]{0,1:T(8,128)(2,1)S(1)}, bf16[1024,768]{0,1:T(8,128)(2,1)}, u32[]{:S(2)}) copy-start(bf16[1024,768]{0,1:T(8,128)(2,1)} %copy-done.3) | copy-start | bytes 4718596
  527.9 8.5 %copy-start.37 = (f32[12,512]{1,0:T(8,128)S(1)}, f32[12,512]{1,0:T(8,128)}, u32[]{:S(2)}) copy-start(f32[12,512]{1,0:T(8,128)} %log_add_fusion) | copy-start | bytes 73732
  527.9 8.5 %copy-start.44 = (f32[12,512]{1,0:T(8,128)S(1)}, f32[12,512]{1,0:T(8,128)}, u32[]{:S(2)}) copy-start(f32[12,512]{1,0:T(8,128)} %get-tuple-element.77) | copy-start | bytes 73732
  578.5 12.2 %copy-start.8 = (bf16[1024,768]{0,1:T(8,128)(2,1)S(1)}, bf16[1024,768]{0,1:T(8,128)(2,1)}, u32[]{:S(2)}) copy-start(bf16[1024,768]{0,1:T(8,128)(2,1)} %copy-done.5) | copy-start | bytes 4718596
  578.5 12.2 %copy-start.55 = (f32[768]{0:T(1024)S(1)}, f32[768]{0:T(1024)}, u32[]{:S(2)}) copy-start(f32[768]{0:T(1024)} %copy-done.54) | copy-start | bytes 9220
  578.5 12.2 %copy-start.57 = (f32[1024]{0:T(1024)S(1)}, f32[1024]{0:T(1024)}, u32[]{:S(2)}) copy-start(f32[1024]{0:T(1024)} %copy-done.56) | copy-start | bytes 12292
  578.5 19.5 %slice-start.3 = ((s8[12582912]{0:T(1024)(128)(4,1)}), s8[4194304]{0:T(1024)(128)(4,1)S(1)}, s32[]{:S(2)}) async-start(s8[12582912]{0:T(1024)(128)(4,1)} %bitcast.163), calls=%async_computation.12 | async-start | bytes 8388608
  578.5 19.5 %slice-start.4 = ((s8[12582912]{0:T(1024)(128)(4,1)}), s8[4194304]{0:T(1024)(128)(4,1)S(1)}, s32[]{:S(2)}) async-start(s8[12582912]{0:T(1024)(128)(4,1)} %bitcast.163), calls=%async_computation.13 | async-start | bytes 8388608
  590.7 4.4 copy-start.33
  590.8 7.3 slice-start.5
  595.2 5.3 slice-start
  595.2 5.3 slice-start.1
  604.6 3.8 copy-start.32
  673.3 3.7 copy-start.53
  677.5 13.1 %copy-start.15 = (s32[512,1024]{0,1:T(8,128)S(1)}, s32[512,1024]{0,1:T(8,128)}, u32[]{:S(2)}) copy-start(s32[512,1024]{0,1:T(8,128)} %fusion.49) | copy-start | bytes 6291460
  690.6 13.5 %copy-start.63 = (f32[768]{0:T(1024)S(1)}, f32[768]{0:T(1024)}, u32[]{:S(2)}) copy-start(f32[768]{0:T(1024)} %get-tuple-element.48) | copy-start | bytes 9220
  (33 other events, 85.5 us)
Sparse Core Ops, SparseCore 0:
  343.5 66.0 reduce-scatter.2
  432.5 61.2 reduce-scatter.4
Sparse Core Ops, SparseCore 1:
  611.3 197.9 all-reduce.3
where the time goes:
time: 837 us; the launch traced here: 827 us
  matrix products  333 us (40%)
  waiting for transfers between devices  150 us (18%)
  local copies, waits for them, and re-layouts  141 us (17%)
  other arithmetic  98.4 us (12%)
  blocking collectives  48 us (6%)
  starting transfers between devices  40.5 us (5%)
  between operations  16.6 us (2%)
    dot_general x2, local copies, waits for them, and re-layouts, score_block(): jnp.einsum('qkb,bh->hqk', onehot, bias_table, preferred_element_type=jnp....  60.8 us
    psum x1, waiting for transfers between devices, local(): lax.psum((gain_one_grad, grad_query_w, grad_key_w, grad_value_w, grad_out...  48.2 us
    psum x1, blocking collectives, local(): lax.psum((gain_one_grad, grad_query_w, grad_key_w, grad_value_w, grad_out...  48 us
    convert_element_type x2, local copies, waits for them, and re-layouts, local(): score_grad_low = (attn_probs * (prob_grad - row_dot)).astype(jnp.bfloat16)  46.5 us
    convert_element_type x2, other arithmetic, local(): score_grad_low = (attn_probs * (prob_grad - row_dot)).astype(jnp.bfloat16)  43 us
    dot_general x2, matrix products, local(): jnp.einsum('qhd,khd->hqk', grad_rows, value_low, preferred_element_type=j...  37.3 us
    dot_general x2, matrix products, score_block(): jnp.einsum('qhd,khd->hqk', query_rows, key_low, preferred_element_type=jn...  34 us
    dot_general x2, matrix products, score_block(): jnp.einsum('qkb,bh->hqk', onehot, bias_table, preferred_element_type=jnp....  32.2 us
  transfers between devices with their start and end apart: 7, of which 5 were waited for; matrix products, arithmetic and copies ran while one was open for 39% of the time, Pallas kernels for 0%

commit v1 on v0

--- a/solution.py
+++ b/solution.py
@@ -253,17 +253,20 @@
     input_resid, gain_one_grad = norm_one_back(normed_grad)
     input_grad = after_grad + input_resid
     summed = lax.psum(
-        (
-            gain_one_grad,
-            grad_query_w,
-            grad_key_w,
-            grad_value_w,
-            grad_output_w,
-            table_grad,
-            gain_two_grad,
-            grad_router,
+        lax.psum(
+            (
+                gain_one_grad,
+                grad_query_w,
+                grad_key_w,
+                grad_value_w,
+                grad_output_w,
+                table_grad,
+                gain_two_grad,
+                grad_router,
+            ),
+            "expert",
         ),
-        ("dp", "expert"),
+        "dp",
     )
     return (
         output,

time: 837 us -> 1020 us (1.22)
  waiting for transfers between devices: 150 us -> 302 us
  blocking collectives: 48 us -> 71.6 us
    psum x1, waiting for transfers between devices: 48.2 us -> 166 us  [local(): lax.psum((gain_one_grad, grad_query_w, grad_key_w, grad_value_w, grad_out...]
    psum x0 -> x1, waiting for transfers between devices: none -> 53.6 us  [local(): lax.psum(lax.psum((gain_one_grad, grad_query_w, grad_key_w, grad_value_w,...]
    all_to_all x1, waiting for transfers between devices: 26.3 us -> 8.44 us  [local(): lax.all_to_all(produced, 'expert', split_axis=1, concat_axis=0, tiled=True)]
    all_to_all x1, waiting for transfers between devices: 26.3 us -> 12.1 us  [local(): lax.all_to_all(slot_grads, 'expert', split_axis=0, concat_axis=1, tiled=T...]
    all_to_all x1, waiting for transfers between devices: 18.4 us -> 31.4 us  [local(): lax.all_to_all(input_grad_low, 'expert', split_axis=1, concat_axis=0, til...]
    psum x1, blocking collectives: 48 us -> 60.6 us  [local(): lax.psum((gain_one_grad, grad_query_w, grad_key_w, grad_value_w, grad_out...]
    psum x0 -> x1, blocking collectives: none -> 11 us  [local(): lax.psum(lax.psum((gain_one_grad, grad_query_w, grad_key_w, grad_value_w,...]
    unnamed x156 -> x164, local copies, waits for them, and re-layouts: 31.9 us -> 36 us
  transfers between devices with their start and end apart: 7 -> 8, of which waited for: 5 -> 6; matrix products, arithmetic and copies ran while one was open for 39% -> 18% of each run, Pallas kernels for 0% -> 0%
where the time goes in v1:
time: 1020 us; the launch traced here: 1010 us
  matrix products  335 us (33%)
  waiting for transfers between devices  302 us (30%)
  local copies, waits for them, and re-layouts  145 us (14%)
  other arithmetic  97.5 us (10%)
  blocking collectives  71.6 us (7%)
  starting transfers between devices  40.5 us (4%)
  between operations  16.7 us (2%)
    psum x1, waiting for transfers between devices, local(): lax.psum((gain_one_grad, grad_query_w, grad_key_w, grad_value_w, grad_out...  166 us
    dot_general x2, local copies, waits for them, and re-layouts, score_block(): jnp.einsum('qkb,bh->hqk', onehot, bias_table, preferred_element_type=jnp....  60.6 us
    psum x1, blocking collectives, local(): lax.psum((gain_one_grad, grad_query_w, grad_key_w, grad_value_w, grad_out...  60.6 us
    psum x1, waiting for transfers between devices, local(): lax.psum(lax.psum((gain_one_grad, grad_query_w, grad_key_w, grad_value_w,...  53.6 us
    convert_element_type x2, local copies, waits for them, and re-layouts, local(): score_grad_low = (attn_probs * (prob_grad - row_dot)).astype(jnp.bfloat16)  46.5 us
    convert_element_type x2, other arithmetic, local(): score_grad_low = (attn_probs * (prob_grad - row_dot)).astype(jnp.bfloat16)  43.3 us
    dot_general x2, matrix products, local(): jnp.einsum('qhd,khd->hqk', grad_rows, value_low, preferred_element_type=j...  38 us
    unnamed x164, local copies, waits for them, and re-layouts  36 us
  transfers between devices with their start and end apart: 8, of which 6 were waited for; matrix products, arithmetic and copies ran while one was open for 18% of the time, Pallas kernels for 0%

profile of v1, /device:TPU:0, one launch (start us, length us, event | category | flops | bytes accessed | tf_op | source)
XLA Modules:
  0.0 1008.4 jit_solution(2521552164683468042)
XLA Ops:
  13.9 4.5 reduce-window.6
  36.9 16.3 %fusion.3 = f32[512,1024,12]{0,2,1:T(8,128)} fusion(s32[512,1024]{0,1:T(8,128)S(1)} %copy-done.15, bf16[32,12]{0,1:T(8,128)(2,1)S(1)} %copy-done.70), kind=kOutput, calls=%fused_computation.5 | convolution fusion | flops 419430400 | bytes 27263744 | tf_op jit(solution)/shard_map/qkb,bh->hqk/dot_general | solution.py:34
  53.2 30.4 %copy.61 = f32[512,1024,12]{1,0,2:T(8,128)} copy(f32[512,1024,12]{0,2,1:T(8,128)} %fusion.3) | data formatting | bytes 50331648 | tf_op jit(solution)/shard_map/qkb,bh->hqk/dot_general | solution.py:34
  83.5 15.8 %fusion.1 = f32[512,1024,12]{0,2,1:T(8,128)} fusion(s32[512,1024]{0,1:T(8,128)} %fusion.49, bf16[32,12]{0,1:T(8,128)(2,1)S(1)} %copy-done.70), kind=kOutput, calls=%fused_computation.2 | convolution fusion | flops 419430400 | bytes 27263744 | tf_op jit(solution)/shard_map/qkb,bh->hqk/dot_general | solution.py:34
  99.3 30.2 %copy.62 = f32[512,1024,12]{1,0,2:T(8,128)} copy(f32[512,1024,12]{0,2,1:T(8,128)} %fusion.1) | data formatting | bytes 50331648 | tf_op jit(solution)/shard_map/qkb,bh->hqk/dot_general | solution.py:34
  129.6 17.0 %fusion.121 = (f32[12,512]{1,0:T(8,128)}, f32[12,512,1024]{2,1,0:T(8,128)}) fusion(f32[512,1024,12]{1,0,2:T(8,128)} %copy.61, bf16[512,12,64]{0,2,1:T(8,128)(2,1)} %bitcast.167, bf16[1024,12,64]{0,2,1:T(8,128)(2,1)S(1)} %bitcast.161), kind=kOutput, calls=%fused_computation.173 | convolution fusion | flops 824174592 | bytes 52715520 | tf_op jit(solution)/shard_map/qhd,khd->hqk/dot_general | solution.py:32
  146.6 11.1 %fusion.8 = f32[12,512]{1,0:T(8,128)S(1)} fusion(f32[12,512,1024]{2,1,0:T(8,128)} %get-tuple-element.77, f32[12,512]{1,0:T(8,128)} %get-tuple-element.76), kind=kLoop, calls=%fused_computation.24 | loop fusion | flops 12576768 | bytes 25214976 | tf_op jit(solution)/shard_map/reduce_sum | solution.py:89
  157.7 11.3 %fusion.84 = bf16[512,12,64]{0,2,1:T(8,128)(2,1)} fusion(bf16[1024,12,64]{0,2,1:T(8,128)(2,1)S(1)} %bitcast.174, f32[12,512,1024]{2,1,0:T(8,128)} %get-tuple-element.77, f32[12,512]{1,0:T(8,128)S(1)} %fusion.8, f32[12,512]{1,0:T(8,128)S(1)} %copy-done.47), kind=kOutput, calls=%fused_computation.128 | convolution fusion | flops 824573952 | bytes 27574272 | tf_op jit(solution)/shard_map/hqk,khd->qhd/dot_general | solution.py:93
  169.0 17.4 %fusion.120 = (f32[12,512]{1,0:T(8,128)}, f32[12,512,1024]{2,1,0:T(8,128)}) fusion(f32[512,1024,12]{1,0,2:T(8,128)} %copy.62, bf16[512,12,64]{0,2,1:T(8,128)(2,1)S(1)} %bitcast.165, bf16[1024,12,64]{0,2,1:T(8,128)(2,1)S(1)} %bitcast.162), kind=kOutput, calls=%fused_computation.172 | convolution fusion | flops 824174592 | bytes 52715520 | tf_op jit(solution)/shard_map/qhd,khd->hqk/dot_general | solution.py:32
  186.4 11.1 %fusion.9 = f32[12,512]{1,0:T(8,128)S(1)} fusion(f32[12,512,1024]{2,1,0:T(8,128)} %get-tuple-element.75, f32[12,512]{1,0:T(8,128)} %get-tuple-element.74), kind=kLoop, calls=%fused_computation.25 | loop fusion | flops 12576768 | bytes 25214976 | tf_op jit(solution)/shard_map/reduce_sum | solution.py:89
  197.5 10.5 %fusion.85 = bf16[512,12,64]{0,2,1:T(8,128)(2,1)S(1)} fusion(bf16[1024,12,64]{0,2,1:T(8,128)(2,1)S(1)} %bitcast.175, f32[12,512,1024]{2,1,0:T(8,128)} %get-tuple-element.75, f32[12,512]{1,0:T(8,128)S(1)} %fusion.9, f32[12,512]{1,0:T(8,128)S(1)} %copy-done.49), kind=kOutput, calls=%fused_computation.129 | convolution fusion | flops 824573952 | bytes 27574272 | tf_op jit(solution)/shard_map/hqk,khd->qhd/dot_general | solution.py:93
  217.5 7.7 all-to-all-start
  228.3 5.3 convolution_convert_fusion
  233.6 30.5 %all-to-all-done = bf16[16,1,80,768]{3,2,1,0:T(8,128)(2,1)} async-done(((bf16[16,1,80,768]{3,2,1,0:T(8,128)(2,1)}), bf16[16,1,80,768]{3,2,1,0:T(8,128)(2,1)}, u32[]{:S(2)}, u32[]{:S(2)}) %all-to-all-start) | async-done | bytes 1966112 | tf_op jit(solution)/shard_map/all_to_all | solution.py:125
  264.1 10.7 %all-to-all-start.2 = ((bf16[16,1,80,768]{3,2,1,0:T(8,128)(2,1)}), bf16[16,1,80,768]{3,2,1,0:T(8,128)(2,1)S(1)}, u32[]{:S(2)}, u32[]{:S(2)}) async-start(bf16[16,1,80,768]{3,2,1,0:T(8,128)(2,1)} %bitcast.182), calls=%async_computation.2 | async-start | bytes 3932160 | tf_op jit(solution)/shard_map/all_to_all | solution.py:148
  274.8 8.7 fusion.33
  283.6 5.5 copy-done.77
  289.0 12.5 %convert_bitcast_fusion.1 = bf16[1,16,80,768]{3,2,0,1:T(8,128)(2,1)} fusion(bf16[1,3072,768]{2,1,0:T(8,128)(2,1)} %param.25, f32[16,80,3072]{2,1,0:T(8,128)S(1)} %fusion.33), kind=kOutput, calls=%fused_computation.113 | convolution fusion | flops 6076170240 | bytes 22413312 | tf_op jit(solution)/shard_map/esrf,efd->esrd/dot_general | solution.py:130
  301.6 12.1 %all-to-all-done.2 = bf16[16,1,80,768]{3,2,1,0:T(8,128)(2,1)S(1)} async-done(((bf16[16,1,80,768]{3,2,1,0:T(8,128)(2,1)}), bf16[16,1,80,768]{3,2,1,0:T(8,128)(2,1)S(1)}, u32[]{:S(2)}, u32[]{:S(2)}) %all-to-all-start.2) | async-done | bytes 1966112 | tf_op jit(solution)/shard_map/all_to_all | solution.py:148
  313.6 11.0 %all-to-all-start.1 = ((bf16[1,16,80,768]{3,2,0,1:T(8,128)(2,1)}), bf16[1,16,80,768]{3,2,0,1:T(8,128)(2,1)}, u32[]{:S(2)}, u32[]{:S(2)}) async-start(bf16[1,16,80,768]{3,2,0,1:T(8,128)(2,1)} %convert_bitcast_fusion.1), calls=%async_computation.1 | async-start | bytes 3932160 | tf_op jit(solution)/shard_map/all_to_all | solution.py:133
  324.6 17.4 %fusion.18 = bf16[16,80,3072]{2,1,0:T(8,128)(2,1)S(1)} fusion(f32[16,80,3072]{2,1,0:T(8,128)} %copy-done.77, bf16[1,3072,768]{2,1,0:T(8,128)(2,1)} %param.25, bf16[16,1,80,768]{3,2,1,0:T(8,128)(2,1)S(1)} %all-to-all-done.2), kind=kOutput, calls=%fused_computation.34 | convolution fusion | flops 6118440960 | bytes 30277632 | tf_op jit(solution)/shard_map/esrd,efd->esrf/dot_general | solution.py:153
  345.2 9.8 convert_bitcast_fusion
  355.0 8.4 all-to-all-done.1
  363.5 10.7 %all-to-all-start.3 = ((bf16[1,16,80,768]{3,2,0,1:T(8,128)(2,1)}), bf16[1,16,80,768]{3,2,0,1:T(8,128)(2,1)}, u32[]{:S(2)}, u32[]{:S(2)}) async-start(bf16[1,16,80,768]{3,2,0,1:T(8,128)(2,1)} %convert_bitcast_fusion), calls=%async_computation.3 | async-start | bytes 3932160 | tf_op jit(solution)/shard_map/all_to_all | solution.py:158
  375.8 5.9 fusion.44
  381.7 31.4 %all-to-all-done.3 = bf16[1,16,80,768]{3,2,0,1:T(8,128)(2,1)} async-done(((bf16[1,16,80,768]{3,2,0,1:T(8,128)(2,1)}), bf16[1,16,80,768]{3,2,0,1:T(8,128)(2,1)}, u32[]{:S(2)}, u32[]{:S(2)}) %all-to-all-start.3) | async-done | bytes 1966112 | tf_op jit(solution)/shard_map/all_to_all | solution.py:158
  427.6 20.7 %multiply_reduce_fusion.1 = (f32[12,512]{1,0:T(8,128)}, f32[12,512,1024]{2,1,0:T(8,128)}) fusion(f32[12,512,1024]{2,1,0:T(8,128)} %get-tuple-element.77, f32[12,512]{1,0:T(8,128)} %log_add_fusion.1, bf16[512,12,64]{0,2,1:T(8,128)(2,1)S(1)} %bitcast.169, bf16[1024,12,64]{0,2,1:T(8,128)(2,1)S(1)} %bitcast.176), kind=kOutput, calls=%fused_computation.16 | convolution fusion | flops 824174592 | bytes 52740096 | tf_op jit(solution)/shard_map/qhd,khd->hqk/dot_general | solution.py:207
  448.3 21.7 %multiply_convert_fusion.1 = bf16[12,512,1024]{2,1,0:T(8,128)(2,1)} fusion(f32[12,512,1024]{2,1,0:T(8,128)} %get-tuple-element.88, f32[12,512,1024]{2,1,0:T(8,128)} %get-tuple-element.77, f32[12,512]{1,0:T(8,128)} %get-tuple-element.87, f32[12,512]{1,0:T(8,128)} %log_add_fusion.1), kind=kLoop, calls=%fused_computation.15 | loop fusion | flops 25165824 | bytes 62963712 | tf_op jit(solution)/shard_map/convert_element_type | solution.py:211
  470.0 9.5 fusion.82
  479.5 8.6 fusion.124
  488.1 12.0 %fusion.19 = f32[12,64,1024]{2,1,0:T(8,128)} fusion(bf16[512,12,64]{0,2,1:T(8,128)(2,1)S(1)} %bitcast.172, f32[12,512,1024]{2,1,0:T(8,128)} %get-tuple-element.75, f32[12,512]{1,0:T(8,128)S(1)} %copy-done.44), kind=kOutput, calls=%fused_computation.36 | convolution fusion | flops 817889280 | bytes 29122560 | tf_op jit(solution)/shard_map/hqk,qhd->khd/dot_general | solution.py:221
  500.1 17.3 %multiply_reduce_fusion = (f32[12,512]{1,0:T(8,128)}, f32[12,512,1024]{2,1,0:T(8,128)}) fusion(f32[12,512,1024]{2,1,0:T(8,128)} %get-tuple-element.75, f32[12,512]{1,0:T(8,128)} %log_add_fusion, bf16[512,12,64]{0,2,1:T(8,128)(2,1)} %bitcast.171, bf16[1024,12,64]{0,2,1:T(8,128)(2,1)} %bitcast.173), kind=kOutput, calls=%fused_computation.13 | convolution fusion | flops 824174592 | bytes 52740096 | tf_op jit(solution)/shard_map/qhd,khd->hqk/dot_general | solution.py:207
  517.3 11.7 %add_convert_fusion = bf16[12,64,1024]{2,1,0:T(8,128)(2,1)S(1)} fusion(f32[12,64,1024]{2,1,0:T(8,128)} %fusion.19, bf16[512,12,64]{0,2,1:T(8,128)(2,1)S(1)} %bitcast.170, f32[12,512,1024]{2,1,0:T(8,128)} %get-tuple-element.77, f32[12,512]{1,0:T(8,128)} %log_add_fusion.1), kind=kOutput, calls=%fused_computation.78 | convolution fusion | flops 819462144 | bytes 30695424 | tf_op jit(solution)/shard_map/hqk,qhd->khd/dot_general | solution.py:221
  531.9 21.6 %multiply_convert_fusion = bf16[12,512,1024]{2,1,0:T(8,128)(2,1)} fusion(f32[12,512,1024]{2,1,0:T(8,128)} %get-tuple-element.86, f32[12,512,1024]{2,1,0:T(8,128)} %get-tuple-element.75, f32[12,512]{1,0:T(8,128)S(1)} %copy-done.52, f32[12,512]{1,0:T(8,128)S(1)} %copy-done.45), kind=kLoop, calls=%fused_computation.12 | loop fusion | flops 25165824 | bytes 62963712 | tf_op jit(solution)/shard_map/convert_element_type | solution.py:211
  553.6 8.6 fusion.83
  562.2 6.9 multiply_convert_fusion.3
  575.2 10.7 %fusion.37 = bf16[1,768,3072]{2,1,0:T(8,128)(2,1)} fusion(bf16[16,80,3072]{2,1,0:T(8,128)(2,1)} %copy-done.76, bf16[16,1,80,768]{3,2,1,0:T(8,128)(2,1)} %all-to-all-done), kind=kOutput, calls=%fused_computation.64 | convolution fusion | flops 6042157056 | bytes 14548992 | tf_op jit(solution)/shard_map/esrd,esrf->edf/dot_general | solution.py:159
  588.0 13.5 %fusion.38 = bf16[1,3072,768]{2,1,0:T(8,128)(2,1)} fusion(bf16[16,1,80,768]{3,2,1,0:T(8,128)(2,1)S(1)} %copy-done.36, f32[16,80,3072]{2,1,0:T(8,128)} %copy-done.77), kind=kOutput, calls=%fused_computation.65 | convolution fusion | flops 6077546496 | bytes 22413312 | tf_op jit(solution)/shard_map/esrf,esrd->efd/dot_general | solution.py:162
  601.6 165.6 %all-reduce.7.cloned.1.call-done = (f32[768,768]{1,0:T(8,128)}, f32[768,768]{1,0:T(8,128)}, f32[768,768]{1,0:T(8,128)}, f32[768,768]{1,0:T(8,128)}) async-done(((f32[768,768]{1,0:T(8,128)}, f32[768,768]{1,0:T(8,128)}, f32[768,768]{1,0:T(8,128)}, f32[768,768]{1,0:T(8,128)}), (f32[768,768]{1,0:T(8,128)}, f32[768,768]{1,0:T(8,128)}, f32[768,768]{1,0:T(8,128)}, ...) | async-done | bytes 9437200 | tf_op jit(solution)/shard_map/psum | solution.py:256
  767.3 23.2 %copy.75 = bf16[12,512,1024]{1,0,2:T(8,128)(2,1)} copy(bf16[12,512,1024]{2,1,0:T(8,128)(2,1)} %multiply_convert_fusion.1) | data formatting | bytes 25165824 | tf_op jit(solution)/shard_map/convert_element_type | solution.py:211
  790.5 23.3 %copy.76 = bf16[12,512,1024]{1,0,2:T(8,128)(2,1)} copy(bf16[12,512,1024]{2,1,0:T(8,128)(2,1)} %multiply_convert_fusion) | data formatting | bytes 25165824 | tf_op jit(solution)/shard_map/convert_element_type | solution.py:211
  829.6 13.1 %fusion.86 = f32[32,12]{0,1:T(8,128)S(1)} fusion(bf16[12,512,1024]{1,0,2:T(8,128)(2,1)} %copy.75, s32[512,1024]{0,1:T(8,128)} %fusion.48), kind=kOutput, calls=%fused_computation.130 | convolution fusion | flops 419430400 | bytes 14681600 | tf_op jit(solution)/shard_map/qkb,hqk->bh/dot_general | solution.py:227
  842.8 13.9 %fusion.88 = f32[32,12]{0,1:T(8,128)S(1)} fusion(f32[32,12]{0,1:T(8,128)S(1)} %fusion.86, bf16[12,512,1024]{1,0,2:T(8,128)(2,1)} %copy.76, s32[512,1024]{0,1:T(8,128)S(1)} %copy-done.16), kind=kOutput, calls=%fused_computation.132 | convolution fusion | flops 419430784 | bytes 14683136 | tf_op jit(solution)/shard_map/qkb,hqk->bh/dot_general | solution.py:227
  856.7 60.6 %all-reduce = (f32[768]{0:T(1024)S(1)}, f32[32,12]{0,1:T(8,128)S(1)}, f32[768]{0:T(1024)S(1)}, f32[768,16]{0,1:T(8,128)S(1)}) all-reduce(f32[768]{0:T(1024)S(1)} %get-tuple-element.50, f32[32,12]{0,1:T(8,128)S(1)} %fusion.88, f32[768]{0:T(1024)S(1)} %copy-done.71, ...), channel_id=1, replica_groups=mesh['dp'=2,'expert'=16] {'expert'}, use_global_device_ids=true, to_apply=%region_18.19 | all-reduce | flops 14208 | bytes 113664 | tf_op jit(solution)/shard_map/psum | solution.py:256
  917.3 11.0 %all-reduce.2 = (f32[768]{0:T(1024)}, f32[32,12]{0,1:T(8,128)}, f32[768]{0:T(1024)}, f32[768,16]{0,1:T(8,128)}) all-reduce(f32[768]{0:T(1024)S(1)} %get-tuple-element.52, f32[32,12]{0,1:T(8,128)S(1)} %get-tuple-element.53, f32[768]{0:T(1024)S(1)} %get-tuple-element.54, ...), channel_id=1, replica_groups=mesh['dp'=2,'expert'=16] {'dp'}, use_global_device_ids=true, to_apply=%region_19.20 | all-reduce | flops 14208 | bytes 113664 | tf_op jit(solution)/shard_map/psum | solution.py:255
  928.3 4.5 convert_element_type.349
  932.8 4.4 convert_element_type.352
  937.2 53.6 %all-reduce.9.cloned.1.call-done = (f32[768,768]{1,0:T(8,128)}, f32[768,768]{1,0:T(8,128)}, f32[768,768]{1,0:T(8,128)}, f32[768,768]{1,0:T(8,128)}) async-done(((f32[768,768]{1,0:T(8,128)}, f32[768,768]{1,0:T(8,128)}, f32[768,768]{1,0:T(8,128)}, f32[768,768]{1,0:T(8,128)}), (f32[768,768]{1,0:T(8,128)}, f32[768,768]{1,0:T(8,128)}, f32[768,768]{1,0:T(8,128)}, ...) | async-done | bytes 9437200 | tf_op jit(solution)/shard_map/psum | solution.py:255
  (224 shorter events, 92.4 us)
Async XLA Ops:
  8.0 22.6 %copy-start = (bf16[768,768]{1,0:T(8,128)(2,1)S(1)}, bf16[768,768]{1,0:T(8,128)(2,1)}, u32[]{:S(2)}) copy-start(bf16[768,768]{1,0:T(8,128)(2,1)} %param.19) | copy-start | bytes 3538948
  10.6 20.0 %copy-start.62 = (f32[768]{0:T(1024)}, f32[768]{0:T(1024)S(1)}, u32[]{:S(2)}) copy-start(f32[768]{0:T(1024)S(1)} %convert_element_type.295) | copy-start | bytes 9220
  22.0 3.8 copy-start.6
  23.0 7.6 copy-start.64
  27.4 141.6 %copy-start.17 = (bf16[512,768]{0,1:T(8,128)(2,1)}, bf16[512,768]{0,1:T(8,128)(2,1)S(1)}, u32[]{:S(2)}) copy-start(bf16[512,768]{0,1:T(8,128)(2,1)S(1)} %get-tuple-element.73) | copy-start | bytes 2359300
  30.7 138.3 %copy-start.4 = (bf16[1024,768]{0,1:T(8,128)(2,1)}, bf16[1024,768]{0,1:T(8,128)(2,1)S(1)}, u32[]{:S(2)}) copy-start(bf16[1024,768]{0,1:T(8,128)(2,1)S(1)} %convolution_convert_fusion.3) | copy-start | bytes 4718596
  30.7 6.2 copy-start.70
  146.6 11.1 %copy-start.21 = (bf16[1024,768]{0,1:T(8,128)(2,1)S(1)}, bf16[1024,768]{0,1:T(8,128)(2,1)}, u32[]{:S(2)}) copy-start(bf16[1024,768]{0,1:T(8,128)(2,1)} %convolution_convert_fusion.5) | copy-start | bytes 4718596
  146.6 11.1 %copy-start.47 = (f32[12,512]{1,0:T(8,128)S(1)}, f32[12,512]{1,0:T(8,128)}, u32[]{:S(2)}) copy-start(f32[12,512]{1,0:T(8,128)} %get-tuple-element.76) | copy-start | bytes 73732
  157.7 11.3 %copy-start.53 = (f32[12,512]{1,0:T(8,128)}, f32[12,512]{1,0:T(8,128)S(1)}, u32[]{:S(2)}) copy-start(f32[12,512]{1,0:T(8,128)S(1)} %fusion.8) | copy-start | bytes 73732
  186.4 11.1 %copy-start.22 = (bf16[1024,768]{0,1:T(8,128)(2,1)S(1)}, bf16[1024,768]{0,1:T(8,128)(2,1)}, u32[]{:S(2)}) copy-start(bf16[1024,768]{0,1:T(8,128)(2,1)} %convolution_convert_fusion.5) | copy-start | bytes 4718596
  186.4 11.1 %copy-start.49 = (f32[12,512]{1,0:T(8,128)S(1)}, f32[12,512]{1,0:T(8,128)}, u32[]{:S(2)}) copy-start(f32[12,512]{1,0:T(8,128)} %get-tuple-element.74) | copy-start | bytes 73732
  197.5 10.5 %copy-start.43 = (bf16[512,12,64]{0,2,1:T(8,128)(2,1)S(1)}, bf16[512,12,64]{0,2,1:T(8,128)(2,1)}, u32[]{:S(2)}) copy-start(bf16[512,12,64]{0,2,1:T(8,128)(2,1)} %fusion.84) | copy-start | bytes 2359300
  208.2 3.8 copy-start.39
  212.8 4.7 copy-start.42
  214.0 13.9 %copy-start.11 = (bf16[1024,768]{0,1:T(8,128)(2,1)}, bf16[1024,768]{0,1:T(8,128)(2,1)S(1)}, u32[]{:S(2)}) copy-start(bf16[1024,768]{0,1:T(8,128)(2,1)S(1)} %multiply_convert_fusion.4) | copy-start | bytes 4718596
  217.5 10.3 %copy-start.57 = (bf16[768,16]{0,1:T(8,128)(2,1)S(1)}, bf16[768,16]{0,1:T(8,128)(2,1)}, u32[]{:S(2)}) copy-start(bf16[768,16]{0,1:T(8,128)(2,1)} %param.23) | copy-start | bytes 73732
  217.5 46.6 %all-to-all-start = ((bf16[16,1,80,768]{3,2,1,0:T(8,128)(2,1)}), bf16[16,1,80,768]{3,2,1,0:T(8,128)(2,1)}, u32[]{:S(2)}, u32[]{:S(2)}) async-start(bf16[16,1,80,768]{3,2,1,0:T(8,128)(2,1)} %bitcast.181), calls=%async_computation | async-start | bytes 3932160 | tf_op jit(solution)/shard_map/all_to_all | solution.py:125
  228.2 189.3 %copy-start.37 = (f32[1024,16]{0,1:T(8,128)}, f32[1024,16]{0,1:T(8,128)S(1)}, u32[]{:S(2)}) copy-start(f32[1024,16]{0,1:T(8,128)S(1)} %get-tuple-element.81) | copy-start | bytes 196612
  228.2 189.3 %copy-start.55 = (f32[1024]{0:T(1024)}, f32[1024]{0:T(1024)S(1)}, u32[]{:S(2)}) copy-start(f32[1024]{0:T(1024)S(1)} %get-tuple-element.80) | copy-start | bytes 12292
  228.2 189.3 %copy-start.60 = (f32[1024]{0:T(1024)}, f32[1024]{0:T(1024)S(1)}, u32[]{:S(2)}) copy-start(f32[1024]{0:T(1024)S(1)} %fusion.101) | copy-start | bytes 12292
  264.1 49.5 %all-to-all-start.2 = ((bf16[16,1,80,768]{3,2,1,0:T(8,128)(2,1)}), bf16[16,1,80,768]{3,2,1,0:T(8,128)(2,1)S(1)}, u32[]{:S(2)}, u32[]{:S(2)}) async-start(bf16[16,1,80,768]{3,2,1,0:T(8,128)(2,1)} %bitcast.182), calls=%async_computation.2 | async-start | bytes 3932160 | tf_op jit(solution)/shard_map/all_to_all | solution.py:148
  283.5 5.5 copy-start.77
  313.6 28.4 %copy-start.35 = (bf16[16,1,80,768]{3,2,1,0:T(8,128)(2,1)}, bf16[16,1,80,768]{3,2,1,0:T(8,128)(2,1)S(1)}, u32[]{:S(2)}) copy-start(bf16[16,1,80,768]{3,2,1,0:T(8,128)(2,1)S(1)} %all-to-all-done.2) | copy-start | bytes 5898244
  313.6 49.8 %all-to-all-start.1 = ((bf16[1,16,80,768]{3,2,0,1:T(8,128)(2,1)}), bf16[1,16,80,768]{3,2,0,1:T(8,128)(2,1)}, u32[]{:S(2)}, u32[]{:S(2)}) async-start(bf16[1,16,80,768]{3,2,0,1:T(8,128)(2,1)} %convert_bitcast_fusion.1), calls=%async_computation.1 | async-start | bytes 3932160 | tf_op jit(solution)/shard_map/all_to_all | solution.py:133
  355.0 19.5 %copy-start.48 = (f32[12,512]{1,0:T(8,128)S(1)}, f32[12,512]{1,0:T(8,128)}, u32[]{:S(2)}) copy-start(f32[12,512]{1,0:T(8,128)} %get-tuple-element.76) | copy-start | bytes 73732
  355.0 19.5 %copy-start.54 = (f32[12,512]{1,0:T(8,128)S(1)}, f32[12,512]{1,0:T(8,128)}, u32[]{:S(2)}) copy-start(f32[12,512]{1,0:T(8,128)} %copy-done.53) | copy-start | bytes 73732
  355.0 20.8 %copy-start.27 = (bf16[1024,768]{0,1:T(8,128)(2,1)S(1)}, bf16[1024,768]{0,1:T(8,128)(2,1)}, u32[]{:S(2)}) copy-start(bf16[1024,768]{0,1:T(8,128)(2,1)} %copy.67) | copy-start | bytes 4718596
  363.5 49.6 %all-to-all-start.3 = ((bf16[1,16,80,768]{3,2,0,1:T(8,128)(2,1)}), bf16[1,16,80,768]{3,2,0,1:T(8,128)(2,1)}, u32[]{:S(2)}, u32[]{:S(2)}) async-start(bf16[1,16,80,768]{3,2,0,1:T(8,128)(2,1)} %convert_bitcast_fusion), calls=%async_computation.3 | async-start | bytes 3932160 | tf_op jit(solution)/shard_map/all_to_all | solution.py:158
  374.2 393.1 %all-reduce.7.cloned.1.call-start = ((), (), s32[]{:S(2)}) async-start(), calls=%async_computation.8 | async-start | bytes 18874368 | tf_op jit(solution)/shard_map/psum | solution.py:256
  381.7 35.9 %copy-start.68 = (f32[1024]{0:T(1024)}, f32[1024]{0:T(1024)S(1)}, u32[]{:S(2)}) copy-start(f32[1024]{0:T(1024)S(1)} %mul.288) | copy-start | bytes 12292
  413.1 4.4 copy-start.2
  448.3 21.7 %copy-start.5 = (bf16[1024,768]{0,1:T(8,128)(2,1)S(1)}, bf16[1024,768]{0,1:T(8,128)(2,1)}, u32[]{:S(2)}) copy-start(bf16[1024,768]{0,1:T(8,128)(2,1)} %copy-done.4) | copy-start | bytes 4718596
  470.0 9.5 copy-start.19
  479.5 8.6 copy-start.20
  479.5 8.6 copy-start.44
  517.3 11.7 %copy-start.9 = (bf16[1024,768]{0,1:T(8,128)(2,1)S(1)}, bf16[1024,768]{0,1:T(8,128)(2,1)}, u32[]{:S(2)}) copy-start(bf16[1024,768]{0,1:T(8,128)(2,1)} %copy-done.6) | copy-start | bytes 4718596
  517.3 11.7 %copy-start.63 = (f32[768]{0:T(1024)S(1)}, f32[768]{0:T(1024)}, u32[]{:S(2)}) copy-start(f32[768]{0:T(1024)} %copy-done.62) | copy-start | bytes 9220
  517.3 11.7 %copy-start.65 = (f32[1024]{0:T(1024)S(1)}, f32[1024]{0:T(1024)}, u32[]{:S(2)}) copy-start(f32[1024]{0:T(1024)} %copy-done.64) | copy-start | bytes 12292
  553.5 8.7 copy-start.3
  553.5 8.7 copy-start.18
  562.2 7.0 copy-start.30
  575.2 353.1 %reduce-scatter.3.cloned.1.call-start = ((), (), s32[]{:S(2)}) async-start(), calls=%async_computation.6 | async-start | bytes 7077888 | tf_op jit(solution)/shard_map/reduce_scatter | solution.py:166
  585.9 346.8 %reduce-scatter.5.cloned.1.call-start = ((), (), s32[]{:S(2)}) async-start(), calls=%async_computation.7 | async-start | bytes 7077888 | tf_op jit(solution)/shard_map/reduce_scatter | solution.py:169
  601.6 389.3 %all-reduce.9.cloned.1.call-start = ((), (), s32[]{:S(2)}) async-start(), calls=%async_computation.9 | async-start | bytes 18874368 | tf_op jit(solution)/shard_map/psum | solution.py:255
  790.5 23.3 %copy-start.26 = (bf16[1024,768]{0,1:T(8,128)(2,1)S(1)}, bf16[1024,768]{0,1:T(8,128)(2,1)}, u32[]{:S(2)}) copy-start(bf16[1024,768]{0,1:T(8,128)(2,1)} %get-tuple-element.69) | copy-start | bytes 4718596
  829.6 13.1 %copy-start.16 = (s32[512,1024]{0,1:T(8,128)S(1)}, s32[512,1024]{0,1:T(8,128)}, u32[]{:S(2)}) copy-start(s32[512,1024]{0,1:T(8,128)} %fusion.49) | copy-start | bytes 6291460
  842.7 13.9 %copy-start.71 = (f32[768]{0:T(1024)S(1)}, f32[768]{0:T(1024)}, u32[]{:S(2)}) copy-start(f32[768]{0:T(1024)} %get-tuple-element.48) | copy-start | bytes 9220
  (38 other events, 101.3 us)
Sparse Core Ops, SparseCore 0:
  575.3 191.9 all-reduce.6
Sparse Core Ops, SparseCore 1:
  586.0 65.9 reduce-scatter.2
  654.3 59.9 reduce-scatter.4
  767.4 223.4 all-reduce.8
